TPU v7x, 256 devices: a whole 4x4x8 slice. The times are simulated.
256 devices in a mesh: section: 16 (over y_hi, z), blk: 16 (over y_lo, x, core).
Axes of the slice: x: 4, y: 4 (y_hi: 2, y_lo: 2; y = y_hi * 2 + y_lo), z: 8, core: 2. Of those that a mesh axis runs over, the one named last changes fastest.
Arguments:
- pending_groups: bfloat16 [1024, 65536], P('section', 'blk'), may hold values from -6 to 6
- coefficient_tiles: bfloat16 [16, 512, 8, 128, 128], P('section', 'blk'), may hold values from -0.25 to 0.25
- source_block_indices: int32 [16, 512, 8], P('section', 'blk'), may hold values from 0 to 511, as said below
- additive_offsets: float32 [16, 65536], P('section', 'blk'), may hold values from -1.75 to 1.75
Outputs:
- emitted: bfloat16 [8, 1024, 65536], P(None, 'section', 'blk')
Inputs may be any that keep to these rules, and one draw needn't show every extreme that they name: `source_block_indices`: within a block-row the 8 block columns are distinct. A block-row held by index d of blk (block-rows d*32 to (d+1)*32 - 1) uses only block columns d*32 - 4 to (d+1)*32 + 3, taken modulo 512; in every layer the first block-row of each index uses column d*32 - 4 and the last uses (d+1)*32 + 3.
All inputs are finite; a program needn't handle non-finite values.
Results may differ from a plain program's by a relative error of at most 0.013.
Values may be sent and summed in bfloat16 or wider, within the bound.
A program may use at most 64 MiB of HBM per device.

v0:
```python
import functools

import jax
import jax.numpy as jnp
from jax import lax
from jax.experimental import pallas as pl
from jax.experimental.pallas import tpu as pltpu
from jax.sharding import PartitionSpec as P

BLK = 128
HALO = 4
TICKS = 8
MESH = pl.DeviceIdType.MESH


def relay_kernel(n_sec, n_blk, cols_ref, pend_ref, w_ref, b_ref, out_ref,
                 slots, work, send_sem, recv_sem, local_sem):
    s = lax.axis_index("section")
    d = lax.axis_index("blk")
    nb = pend_ref.shape[0]
    npad = nb + 2 * HALO
    left = lax.rem(d + n_blk - 1, n_blk)
    right = lax.rem(d + 1, n_blk)
    s_next = jnp.minimum(s + 1, n_sec - 1)
    s_prev = jnp.maximum(s - 1, 0)

    barrier = pltpu.get_barrier_semaphore()
    for nd in (left, right):
        pl.semaphore_signal(barrier, inc=1, device_id=(s, nd), device_id_type=MESH)

    @pl.when(s < n_sec - 1)
    def _():
        for nd in (left, d, right):
            pl.semaphore_signal(barrier, inc=1, device_id=(s_next, nd), device_id_type=MESH)

    @pl.when(s > 0)
    def _():
        for nd in (left, d, right):
            pl.semaphore_signal(barrier, inc=1, device_id=(s_prev, nd), device_id_type=MESH)

    has_prev = (s + n_sec - 1) // n_sec
    has_next = (2 * n_sec - 3 - s) // (n_sec - 1)
    pl.semaphore_wait(barrier, 2 + 3 * has_prev + 3 * has_next)

    def edge_copies(src, t, tgt_sec):
        lo = pltpu.make_async_remote_copy(
            src_ref=src.at[pl.ds(0, HALO)],
            dst_ref=slots.at[t, pl.ds(HALO + nb, HALO)],
            send_sem=send_sem.at[t, 1], recv_sem=recv_sem.at[t, 1],
            device_id=(tgt_sec, left), device_id_type=MESH)
        hi = pltpu.make_async_remote_copy(
            src_ref=src.at[pl.ds(nb - HALO, HALO)],
            dst_ref=slots.at[t, pl.ds(0, HALO)],
            send_sem=send_sem.at[t, 2], recv_sem=recv_sem.at[t, 2],
            device_id=(tgt_sec, right), device_id_type=MESH)
        return lo, hi

    def center_copy(src, t, tgt_sec):
        return pltpu.make_async_remote_copy(
            src_ref=src,
            dst_ref=slots.at[t, pl.ds(HALO, nb)],
            send_sem=send_sem.at[t, 0], recv_sem=recv_sem.at[t, 0],
            device_id=(tgt_sec, d), device_id_type=MESH)

    lo0, hi0 = edge_copies(pend_ref, 0, s)
    lo0.start()
    hi0.start()
    own = pltpu.make_async_copy(pend_ref, work.at[pl.ds(HALO, nb)], local_sem.at[0])
    own.start()
    own.wait()
    lo0.wait_recv()
    hi0.wait_recv()
    cp_lo = pltpu.make_async_copy(slots.at[0, pl.ds(0, HALO)], work.at[pl.ds(0, HALO)], local_sem.at[1])
    cp_hi = pltpu.make_async_copy(slots.at[0, pl.ds(HALO + nb, HALO)], work.at[pl.ds(HALO + nb, HALO)],
                                  local_sem.at[2])
    cp_lo.start()
    cp_hi.start()
    cp_lo.wait()
    cp_hi.wait()

    def compute(t):
        def row_body(i, carry):
            xs = [work[cols_ref[i, k]] for k in range(w_ref.shape[1] // BLK)]
            xcat = jnp.concatenate(xs, axis=1)
            acc = jnp.dot(xcat, w_ref[i], preferred_element_type=jnp.float32)
            acc = acc + b_ref[i]
            out_ref[t, i] = jnp.maximum(acc, 0.0).astype(out_ref.dtype)
            return carry
        lax.fori_loop(0, nb, row_body, 0)

    for t in range(TICKS):
        if t > 0:
            @pl.when(s >= t)
            def _():
                c = center_copy(out_ref.at[t - 1], t, s)
                lo, hi = edge_copies(out_ref.at[t - 1], t, s)
                c.wait_recv()
                lo.wait_recv()
                hi.wait_recv()
                cw = pltpu.make_async_copy(slots.at[t], work, local_sem.at[0])
                cw.start()
                cw.wait()

        @pl.when(s >= t)
        def _():
            compute(t)

        @pl.when(s < t)
        def _():
            out_ref[t] = jnp.zeros(out_ref.shape[1:], out_ref.dtype)

        if t + 1 < TICKS:
            @pl.when((s >= t) & (s < n_sec - 1))
            def _():
                c = center_copy(out_ref.at[t], t + 1, s_next)
                lo, hi = edge_copies(out_ref.at[t], t + 1, s_next)
                c.start()
                lo.start()
                hi.start()

    lo0.wait_send()
    hi0.wait_send()
    for t in range(TICKS - 1):
        @pl.when((s >= t) & (s < n_sec - 1))
        def _():
            c = center_copy(out_ref.at[t], t + 1, s_next)
            lo, hi = edge_copies(out_ref.at[t], t + 1, s_next)
            c.wait_send()
            lo.wait_send()
            hi.wait_send()


def shards(n_sec, n_blk, pending_groups, coefficient_tiles, source_block_indices, additive_offsets):
    rows, units = pending_groups.shape
    nb = coefficient_tiles.shape[1]
    nz = coefficient_tiles.shape[2]
    d = lax.axis_index("blk")
    cols = jnp.mod(source_block_indices[0] - d * nb + HALO, nb * n_blk).astype(jnp.int32)
    pend = pending_groups.reshape(rows, nb, BLK).transpose(1, 0, 2)
    w = coefficient_tiles[0].reshape(nb, nz * BLK, BLK)
    bias = additive_offsets[0].reshape(nb, 1, BLK)
    npad = nb + 2 * HALO
    out = pl.pallas_call(
        functools.partial(relay_kernel, n_sec, n_blk),
        out_shape=jax.ShapeDtypeStruct((TICKS, nb, rows, BLK), jnp.bfloat16),
        in_specs=[
            pl.BlockSpec(memory_space=pltpu.SMEM),
            pl.BlockSpec(memory_space=pltpu.VMEM),
            pl.BlockSpec(memory_space=pltpu.VMEM),
            pl.BlockSpec(memory_space=pltpu.VMEM),
        ],
        out_specs=pl.BlockSpec(memory_space=pltpu.VMEM),
        scratch_shapes=[
            pltpu.VMEM((TICKS, npad, rows, BLK), jnp.bfloat16),
            pltpu.VMEM((npad, rows, BLK), jnp.bfloat16),
            pltpu.SemaphoreType.DMA((TICKS, 3)),
            pltpu.SemaphoreType.DMA((TICKS, 3)),
            pltpu.SemaphoreType.DMA((3,)),
        ],
        compiler_params=pltpu.CompilerParams(
            collective_id=0, has_side_effects=True, vmem_limit_bytes=48 * 1024 * 1024),
    )(cols, pend, w, bias)
    return out.transpose(0, 2, 1, 3).reshape(TICKS, rows, nb * BLK)


def solution(mesh):
    n_sec = mesh.shape["section"]
    n_blk = mesh.shape["blk"]
    in_specs = (
        P("section", "blk"),
        P("section", "blk", None, None, None),
        P("section", "blk", None),
        P("section", "blk"),
    )
    out_specs = P(None, "section", "blk")
    return jax.shard_map(functools.partial(shards, n_sec, n_blk), mesh=mesh, in_specs=in_specs,
                         out_specs=out_specs, check_vma=False)
```

profile of v0, /device:TPU:16, one launch (start us, length us, event | category | flops | bytes accessed | tf_op | source)
XLA Modules:
  0.0 176.0 jit_solution(1528096275751936597)
XLA Ops:
  0.0 0.0 copy-start
  0.0 0.8 copy.9
  0.8 0.2 copy-done
  1.1 0.1 bitcast_bitcast_fusion.pend_ref
  1.2 0.0 copy-start.1
  1.2 0.7 copy-done.1
  1.9 171.4 %shard_map.46 = bf16[8,32,64,128]{3,2,1,0:T(8,128)(2,1)S(1)} custom-call(s32[32,8]{1,0:T(8,128)S(1)} %add_select_fusion.cols_ref, bf16[32,64,128]{2,1,0:T(8,128)(2,1)S(1)} %bitcast_bitcast_fusion.pend_ref, bf16[32,1024,128]{2,1,0:T(8,128)(2,1)} %bitcast.20, f32[32,1,128]{2,1,0:T(1,128)S(1)} %bitcast.19), custom_call_target="tpu_custom_call" | custom-call | tf_op jit(solution)/shard_map/pallas_call | solution.py:143
  173.3 2.7 %copy_bitcast_fusion = bf16[8,64,4096]{2,1,0:T(8,128)(2,1)} fusion(bf16[8,32,64,128]{3,2,1,0:T(8,128)(2,1)S(1)} %shard_map.46), kind=kLoop, calls=%fused_computation | loop fusion | bytes 8388608 | tf_op jit(solution)/shard_map/reshape | solution.py:163
  (1 shorter events, 0.0 us)
Async XLA Ops:
  0.0 1.1 copy-start
  1.2 0.7 copy-start.1
where the time goes:
time: 179 us; the launch traced here: 176 us
  Pallas kernels  171 us (96%)
  local copies, waits for them, and re-layouts  4.57 us (3%)
    pallas_call x1, Pallas kernels, shards(): pl.pallas_call(functools.partial(relay_kernel, n_sec, n_blk), out_shape=j...  171 us

commit v1 on v0

v1 whole, which is shorter than its diff:
```python
import functools

import jax
import jax.numpy as jnp
from jax import lax
from jax.experimental import pallas as pl
from jax.experimental.pallas import tpu as pltpu
from jax.sharding import PartitionSpec as P

BLK = 128
HALO = 4
TICKS = 8
ROW_CHUNKS = 2
MESH = pl.DeviceIdType.MESH


def relay_kernel(n_sec, n_blk, n_chunk, cols_ref, pend_ref, w_ref, b_ref, out_ref,
                 slots, send_sem, recv_sem, local_sem, *works):
    s = lax.axis_index("section")
    d = lax.axis_index("blk")
    nb = pend_ref.shape[0]
    rc = pend_ref.shape[1] // n_chunk
    left = lax.rem(d + n_blk - 1, n_blk)
    right = lax.rem(d + 1, n_blk)
    s_next = jnp.minimum(s + 1, n_sec - 1)
    s_prev = jnp.maximum(s - 1, 0)

    barrier = pltpu.get_barrier_semaphore()
    for nd in (left, right):
        pl.semaphore_signal(barrier, inc=1, device_id=(s, nd), device_id_type=MESH)

    @pl.when(s < n_sec - 1)
    def _():
        for nd in (left, d, right):
            pl.semaphore_signal(barrier, inc=1, device_id=(s_next, nd), device_id_type=MESH)

    @pl.when(s > 0)
    def _():
        for nd in (left, d, right):
            pl.semaphore_signal(barrier, inc=1, device_id=(s_prev, nd), device_id_type=MESH)

    has_prev = (s + n_sec - 1) // n_sec
    has_next = (2 * n_sec - 3 - s) // (n_sec - 1)
    pl.semaphore_wait(barrier, 2 + 3 * has_prev + 3 * has_next)

    def copies(src, t, c, tgt_sec):
        rows = pl.ds(c * rc, rc)
        center = pltpu.make_async_remote_copy(
            src_ref=src.at[:, rows],
            dst_ref=slots.at[t, pl.ds(HALO, nb), rows],
            send_sem=send_sem.at[t, c, 0], recv_sem=recv_sem.at[t, c, 0],
            device_id=(tgt_sec, d), device_id_type=MESH)
        lo = pltpu.make_async_remote_copy(
            src_ref=src.at[pl.ds(0, HALO), rows],
            dst_ref=slots.at[t, pl.ds(HALO + nb, HALO), rows],
            send_sem=send_sem.at[t, c, 1], recv_sem=recv_sem.at[t, c, 1],
            device_id=(tgt_sec, left), device_id_type=MESH)
        hi = pltpu.make_async_remote_copy(
            src_ref=src.at[pl.ds(nb - HALO, HALO), rows],
            dst_ref=slots.at[t, pl.ds(0, HALO), rows],
            send_sem=send_sem.at[t, c, 2], recv_sem=recv_sem.at[t, c, 2],
            device_id=(tgt_sec, right), device_id_type=MESH)
        return center, lo, hi

    first = [copies(pend_ref, 0, c, s)[1:] for c in range(n_chunk)]
    for pair in first:
        for cp in pair:
            cp.start()
    for c in range(n_chunk):
        rows = pl.ds(c * rc, rc)
        own = pltpu.make_async_copy(pend_ref.at[:, rows], works[c].at[pl.ds(HALO, nb)], local_sem.at[0])
        own.start()
        own.wait()
        for cp in first[c]:
            cp.wait_recv()
        cp_lo = pltpu.make_async_copy(slots.at[0, pl.ds(0, HALO), rows], works[c].at[pl.ds(0, HALO)],
                                      local_sem.at[1])
        cp_hi = pltpu.make_async_copy(slots.at[0, pl.ds(HALO + nb, HALO), rows],
                                      works[c].at[pl.ds(HALO + nb, HALO)], local_sem.at[2])
        cp_lo.start()
        cp_hi.start()
        cp_lo.wait()
        cp_hi.wait()

    def compute(t, c):
        work = works[c]

        def row_body(i, carry):
            xs = [work[cols_ref[i, k]] for k in range(w_ref.shape[1] // BLK)]
            xcat = jnp.concatenate(xs, axis=1)
            acc = jnp.dot(xcat, w_ref[i], preferred_element_type=jnp.float32)
            acc = acc + b_ref[i]
            out_ref[t, i, pl.ds(c * rc, rc)] = jnp.maximum(acc, 0.0).astype(out_ref.dtype)
            return carry
        lax.fori_loop(0, nb, row_body, 0)

    for t in range(TICKS):
        for c in range(n_chunk):
            if t > 0:
                @pl.when(s >= t)
                def _():
                    for cp in copies(out_ref.at[t - 1], t, c, s):
                        cp.wait_recv()
                    cw = pltpu.make_async_copy(slots.at[t, :, pl.ds(c * rc, rc)], works[c], local_sem.at[0])
                    cw.start()
                    cw.wait()

            @pl.when(s >= t)
            def _():
                compute(t, c)

            @pl.when(s < t)
            def _():
                out_ref[t, :, pl.ds(c * rc, rc)] = jnp.zeros((nb, rc, BLK), out_ref.dtype)

            if t + 1 < TICKS:
                @pl.when((s >= t) & (s < n_sec - 1))
                def _():
                    for cp in copies(out_ref.at[t], t + 1, c, s_next):
                        cp.start()

    for pair in first:
        for cp in pair:
            cp.wait_send()
    for t in range(TICKS - 1):
        @pl.when((s >= t) & (s < n_sec - 1))
        def _():
            for c in range(n_chunk):
                for cp in copies(out_ref.at[t], t + 1, c, s_next):
                    cp.wait_send()


def shards(n_sec, n_blk, n_chunk, pending_groups, coefficient_tiles, source_block_indices, additive_offsets):
    rows, units = pending_groups.shape
    nb = coefficient_tiles.shape[1]
    nz = coefficient_tiles.shape[2]
    d = lax.axis_index("blk")
    cols = jnp.mod(source_block_indices[0] - d * nb + HALO, nb * n_blk).astype(jnp.int32)
    pend = pending_groups.reshape(rows, nb, BLK).transpose(1, 0, 2)
    w = coefficient_tiles[0].reshape(nb, nz * BLK, BLK)
    bias = additive_offsets[0].reshape(nb, 1, BLK)
    npad = nb + 2 * HALO
    out = pl.pallas_call(
        functools.partial(relay_kernel, n_sec, n_blk, n_chunk),
        out_shape=jax.ShapeDtypeStruct((TICKS, nb, rows, BLK), jnp.bfloat16),
        in_specs=[
            pl.BlockSpec(memory_space=pltpu.SMEM),
            pl.BlockSpec(memory_space=pltpu.VMEM),
            pl.BlockSpec(memory_space=pltpu.VMEM),
            pl.BlockSpec(memory_space=pltpu.VMEM),
        ],
        out_specs=pl.BlockSpec(memory_space=pltpu.VMEM),
        scratch_shapes=[
            pltpu.VMEM((TICKS, npad, rows, BLK), jnp.bfloat16),
            pltpu.SemaphoreType.DMA((TICKS, n_chunk, 3)),
            pltpu.SemaphoreType.DMA((TICKS, n_chunk, 3)),
            pltpu.SemaphoreType.DMA((3,)),
        ] + [pltpu.VMEM((npad, rows // n_chunk, BLK), jnp.bfloat16) for _ in range(n_chunk)],
        compiler_params=pltpu.CompilerParams(
            collective_id=0, has_side_effects=True, vmem_limit_bytes=48 * 1024 * 1024),
    )(cols, pend, w, bias)
    return out.transpose(0, 2, 1, 3).reshape(TICKS, rows, nb * BLK)


def solution(mesh):
    n_sec = mesh.shape["section"]
    n_blk = mesh.shape["blk"]
    in_specs = (
        P("section", "blk"),
        P("section", "blk", None, None, None),
        P("section", "blk", None),
        P("section", "blk"),
    )
    out_specs = P(None, "section", "blk")
    return jax.shard_map(functools.partial(shards, n_sec, n_blk, ROW_CHUNKS), mesh=mesh, in_specs=in_specs,
                         out_specs=out_specs, check_vma=False)
```

time: 179 us -> 138 us (0.77)
  Pallas kernels: 171 us -> 132 us
    pallas_call x1, Pallas kernels: 171 us -> 132 us  [shards(): pl.pallas_call(functools.partial(relay_kernel, n_sec, n_blk, n_chunk), ou...]
where the time goes in v1:
time: 138 us; the launch traced here: 137 us
  Pallas kernels  132 us (96%)
  local copies, waits for them, and re-layouts  4.57 us (3%)
    pallas_call x1, Pallas kernels, shards(): pl.pallas_call(functools.partial(relay_kernel, n_sec, n_blk, n_chunk), ou...  132 us

profile of v1, /device:TPU:16, one launch (start us, length us, event | category | flops | bytes accessed | tf_op | source)
XLA Modules:
  0.0 136.5 jit_solution(17504467330200934255)
XLA Ops:
  0.0 0.0 copy-start
  0.0 0.8 copy.9
  0.8 0.2 copy-done
  1.1 0.1 bitcast_bitcast_fusion.pend_ref
  1.2 0.0 copy-start.1
  1.2 0.7 copy-done.1
  1.9 131.9 %shard_map.46 = bf16[8,32,64,128]{3,2,1,0:T(8,128)(2,1)S(1)} custom-call(s32[32,8]{1,0:T(8,128)S(1)} %add_select_fusion.cols_ref, bf16[32,64,128]{2,1,0:T(8,128)(2,1)S(1)} %bitcast_bitcast_fusion.pend_ref, bf16[32,1024,128]{2,1,0:T(8,128)(2,1)} %bitcast.20, f32[32,1,128]{2,1,0:T(1,128)S(1)} %bitcast.19), custom_call_target="tpu_custom_call" | custom-call | tf_op jit(solution)/shard_map/pallas_call | solution.py:143
  133.8 2.7 %copy_bitcast_fusion = bf16[8,64,4096]{2,1,0:T(8,128)(2,1)} fusion(bf16[8,32,64,128]{3,2,1,0:T(8,128)(2,1)S(1)} %shard_map.46), kind=kLoop, calls=%fused_computation | loop fusion | bytes 8388608 | tf_op jit(solution)/shard_map/reshape | solution.py:162
  (1 shorter events, 0.0 us)
Async XLA Ops:
  0.0 1.1 copy-start
  1.2 0.7 copy-start.1

commit v2 on v1

--- a/solution.py
+++ b/solution.py
@@ -10,7 +10,7 @@
 BLK = 128
 HALO = 4
 TICKS = 8
-ROW_CHUNKS = 2
+ROW_CHUNKS = 4
 MESH = pl.DeviceIdType.MESH
 
 

time: 138 us -> 184 us (1.33)
  Pallas kernels: 132 us -> 179 us
    pallas_call x1, Pallas kernels: 132 us -> 179 us  [shards(): pl.pallas_call(functools.partial(relay_kernel, n_sec, n_blk, n_chunk), ou...]
where the time goes in v2:
time: 184 us
  Pallas kernels  179 us (97%)
  local copies, waits for them, and re-layouts  4.57 us (2%)
    pallas_call x1, Pallas kernels, shards(): pl.pallas_call(functools.partial(relay_kernel, n_sec, n_blk, n_chunk), ou...  179 us

profile of v2, /device:TPU:16, one launch (start us, length us, event | category | flops | bytes accessed | tf_op | source)
XLA Modules:
  0.0 183.6 jit_solution(10526513568083895075)
XLA Ops:
  0.0 0.0 copy-start
  0.0 0.8 copy.9
  0.8 0.2 copy-done
  1.1 0.1 bitcast_bitcast_fusion.pend_ref
  1.2 0.0 copy-start.1
  1.2 0.7 copy-done.1
  1.9 179.0 %shard_map.46 = bf16[8,32,64,128]{3,2,1,0:T(8,128)(2,1)S(1)} custom-call(s32[32,8]{1,0:T(8,128)S(1)} %add_select_fusion.cols_ref, bf16[32,64,128]{2,1,0:T(8,128)(2,1)S(1)} %bitcast_bitcast_fusion.pend_ref, bf16[32,1024,128]{2,1,0:T(8,128)(2,1)} %bitcast.20, f32[32,1,128]{2,1,0:T(1,128)S(1)} %bitcast.19), custom_call_target="tpu_custom_call" | custom-call | tf_op jit(solution)/shard_map/pallas_call | solution.py:143
  180.9 2.7 %copy_bitcast_fusion = bf16[8,64,4096]{2,1,0:T(8,128)(2,1)} fusion(bf16[8,32,64,128]{3,2,1,0:T(8,128)(2,1)S(1)} %shard_map.46), kind=kLoop, calls=%fused_computation | loop fusion | bytes 8388608 | tf_op jit(solution)/shard_map/reshape | solution.py:162
  (1 shorter events, 0.0 us)
Async XLA Ops:
  0.0 1.1 copy-start
  1.2 0.7 copy-start.1

commit v3 on v1

--- a/solution.py
+++ b/solution.py
@@ -92,7 +92,7 @@
             acc = acc + b_ref[i]
             out_ref[t, i, pl.ds(c * rc, rc)] = jnp.maximum(acc, 0.0).astype(out_ref.dtype)
             return carry
-        lax.fori_loop(0, nb, row_body, 0)
+        lax.fori_loop(0, nb, row_body, 0, unroll=8)
 
     for t in range(TICKS):
         for c in range(n_chunk):

time: 138 us -> 127 us (0.920); the launches traced: 137 us -> 127 us
  Pallas kernels: 132 us -> 123 us
    pallas_call x1, Pallas kernels: 132 us -> 123 us  [shards(): pl.pallas_call(functools.partial(relay_kernel, n_sec, n_blk, n_chunk), ou...]
where the time goes in v3:
time: 127 us
  Pallas kernels  123 us (97%)
  local copies, waits for them, and re-layouts  4.57 us (4%)
    pallas_call x1, Pallas kernels, shards(): pl.pallas_call(functools.partial(relay_kernel, n_sec, n_blk, n_chunk), ou...  123 us
    reshape x1, local copies, waits for them, and re-layouts, shards(): return out.transpose(0, 2, 1, 3).reshape(TICKS, rows, nb * BLK)  2.68 us

profile of v3, /device:TPU:16, one launch (start us, length us, event | category | flops | bytes accessed | tf_op | source)
XLA Modules:
  0.0 127.3 jit_solution(7195539867978312004)
XLA Ops:
  0.0 0.0 copy-start
  0.0 0.8 copy.9
  0.8 0.2 copy-done
  1.1 0.1 bitcast_bitcast_fusion.pend_ref
  1.2 0.0 copy-start.1
  1.2 0.7 copy-done.1
  1.9 122.7 %shard_map.46 = bf16[8,32,64,128]{3,2,1,0:T(8,128)(2,1)S(1)} custom-call(s32[32,8]{1,0:T(8,128)S(1)} %add_select_fusion.cols_ref, bf16[32,64,128]{2,1,0:T(8,128)(2,1)S(1)} %bitcast_bitcast_fusion.pend_ref, bf16[32,1024,128]{2,1,0:T(8,128)(2,1)} %bitcast.20, f32[32,1,128]{2,1,0:T(1,128)S(1)} %bitcast.19), custom_call_target="tpu_custom_call" | custom-call | tf_op jit(solution)/shard_map/pallas_call | solution.py:143
  124.6 2.7 %copy_bitcast_fusion = bf16[8,64,4096]{2,1,0:T(8,128)(2,1)} fusion(bf16[8,32,64,128]{3,2,1,0:T(8,128)(2,1)S(1)} %shard_map.46), kind=kLoop, calls=%fused_computation | loop fusion | bytes 8388608 | tf_op jit(solution)/shard_map/reshape | solution.py:162
  (1 shorter events, 0.0 us)
Async XLA Ops:
  0.0 1.1 copy-start
  1.2 0.7 copy-start.1

commit v4 on v3

--- a/solution.py
+++ b/solution.py
@@ -31,38 +31,39 @@
 
     @pl.when(s < n_sec - 1)
     def _():
-        for nd in (left, d, right):
-            pl.semaphore_signal(barrier, inc=1, device_id=(s_next, nd), device_id_type=MESH)
+        pl.semaphore_signal(barrier, inc=1, device_id=(s_next, d), device_id_type=MESH)
 
     @pl.when(s > 0)
     def _():
-        for nd in (left, d, right):
-            pl.semaphore_signal(barrier, inc=1, device_id=(s_prev, nd), device_id_type=MESH)
+        pl.semaphore_signal(barrier, inc=1, device_id=(s_prev, d), device_id_type=MESH)
 
     has_prev = (s + n_sec - 1) // n_sec
     has_next = (2 * n_sec - 3 - s) // (n_sec - 1)
-    pl.semaphore_wait(barrier, 2 + 3 * has_prev + 3 * has_next)
+    pl.semaphore_wait(barrier, 2 + has_prev + has_next)
 
-    def copies(src, t, c, tgt_sec):
+    def center_copy(t, c):
         rows = pl.ds(c * rc, rc)
-        center = pltpu.make_async_remote_copy(
-            src_ref=src.at[:, rows],
+        return pltpu.make_async_remote_copy(
+            src_ref=out_ref.at[t - 1, :, rows],
             dst_ref=slots.at[t, pl.ds(HALO, nb), rows],
             send_sem=send_sem.at[t, c, 0], recv_sem=recv_sem.at[t, c, 0],
-            device_id=(tgt_sec, d), device_id_type=MESH)
+            device_id=(s_next, d), device_id_type=MESH)
+
+    def edge_copies(src, t, c):
+        rows = pl.ds(c * rc, rc)
         lo = pltpu.make_async_remote_copy(
             src_ref=src.at[pl.ds(0, HALO), rows],
             dst_ref=slots.at[t, pl.ds(HALO + nb, HALO), rows],
             send_sem=send_sem.at[t, c, 1], recv_sem=recv_sem.at[t, c, 1],
-            device_id=(tgt_sec, left), device_id_type=MESH)
+            device_id=(s, left), device_id_type=MESH)
         hi = pltpu.make_async_remote_copy(
             src_ref=src.at[pl.ds(nb - HALO, HALO), rows],
             dst_ref=slots.at[t, pl.ds(0, HALO), rows],
             send_sem=send_sem.at[t, c, 2], recv_sem=recv_sem.at[t, c, 2],
-            device_id=(tgt_sec, right), device_id_type=MESH)
-        return center, lo, hi
+            device_id=(s, right), device_id_type=MESH)
+        return lo, hi
 
-    first = [copies(pend_ref, 0, c, s)[1:] for c in range(n_chunk)]
+    first = [edge_copies(pend_ref, 0, c) for c in range(n_chunk)]
     for pair in first:
         for cp in pair:
             cp.start()
@@ -99,7 +100,11 @@
             if t > 0:
                 @pl.when(s >= t)
                 def _():
-                    for cp in copies(out_ref.at[t - 1], t, c, s):
+                    center_copy(t, c).wait_recv()
+                    fwd = edge_copies(slots.at[t, pl.ds(HALO, nb)], t, c)
+                    for cp in fwd:
+                        cp.start()
+                    for cp in fwd:
                         cp.wait_recv()
                     cw = pltpu.make_async_copy(slots.at[t, :, pl.ds(c * rc, rc)], works[c], local_sem.at[0])
                     cw.start()
@@ -116,8 +121,7 @@
             if t + 1 < TICKS:
                 @pl.when((s >= t) & (s < n_sec - 1))
                 def _():
-                    for cp in copies(out_ref.at[t], t + 1, c, s_next):
-                        cp.start()
+                    center_copy(t + 1, c).start()
 
     for pair in first:
         for cp in pair:
@@ -126,7 +130,12 @@
         @pl.when((s >= t) & (s < n_sec - 1))
         def _():
             for c in range(n_chunk):
-                for cp in copies(out_ref.at[t], t + 1, c, s_next):
+                center_copy(t + 1, c).wait_send()
+    for t in range(1, TICKS):
+        @pl.when(s >= t)
+        def _():
+            for c in range(n_chunk):
+                for cp in edge_copies(slots.at[t, pl.ds(HALO, nb)], t, c):
                     cp.wait_send()
 
 

time: 127 us -> 111 us (0.87)
  Pallas kernels: 123 us -> 106 us
    pallas_call x1, Pallas kernels: 123 us -> 106 us  [shards(): pl.pallas_call(functools.partial(relay_kernel, n_sec, n_blk, n_chunk), ou...]
where the time goes in v4:
time: 111 us
  Pallas kernels  106 us (95%)
  local copies, waits for them, and re-layouts  4.57 us (4%)
    pallas_call x1, Pallas kernels, shards(): pl.pallas_call(functools.partial(relay_kernel, n_sec, n_blk, n_chunk), ou...  106 us
    reshape x1, local copies, waits for them, and re-layouts, shards(): return out.transpose(0, 2, 1, 3).reshape(TICKS, rows, nb * BLK)  2.68 us

profile of v4, /device:TPU:16, one launch (start us, length us, event | category | flops | bytes accessed | tf_op | source)
XLA Modules:
  0.0 110.8 jit_solution(5866076081086760424)
XLA Ops:
  0.0 0.0 copy-start
  0.0 0.8 copy.9
  0.8 0.2 copy-done
  1.1 0.1 bitcast_bitcast_fusion.pend_ref
  1.2 0.0 copy-start.1
  1.2 0.7 copy-done.1
  1.9 106.1 %shard_map.46 = bf16[8,32,64,128]{3,2,1,0:T(8,128)(2,1)S(1)} custom-call(s32[32,8]{1,0:T(8,128)S(1)} %add_select_fusion.cols_ref, bf16[32,64,128]{2,1,0:T(8,128)(2,1)S(1)} %bitcast_bitcast_fusion.pend_ref, bf16[32,1024,128]{2,1,0:T(8,128)(2,1)} %bitcast.20, f32[32,1,128]{2,1,0:T(1,128)S(1)} %bitcast.19), custom_call_target="tpu_custom_call" | custom-call | tf_op jit(solution)/shard_map/pallas_call | solution.py:152
  108.1 2.7 %copy_bitcast_fusion = bf16[8,64,4096]{2,1,0:T(8,128)(2,1)} fusion(bf16[8,32,64,128]{3,2,1,0:T(8,128)(2,1)S(1)} %shard_map.46), kind=kLoop, calls=%fused_computation | loop fusion | bytes 8388608 | tf_op jit(solution)/shard_map/reshape | solution.py:171
  (1 shorter events, 0.0 us)
Async XLA Ops:
  0.0 1.1 copy-start
  1.2 0.7 copy-start.1

commit v5 on v4

--- a/solution.py
+++ b/solution.py
@@ -11,11 +11,19 @@
 HALO = 4
 TICKS = 8
 ROW_CHUNKS = 2
+W_PIECES = 4
 MESH = pl.DeviceIdType.MESH
 
 
-def relay_kernel(n_sec, n_blk, n_chunk, cols_ref, pend_ref, w_ref, b_ref, out_ref,
-                 slots, send_sem, recv_sem, local_sem, *works):
+def relay_kernel(n_sec, n_blk, n_chunk, cols_ref, pend_ref, w_hbm, b_ref, out_ref,
+                 w_ref, w_sem, slots, send_sem, recv_sem, local_sem, *works):
+    n_piece = w_sem.shape[0]
+    per_piece = w_hbm.shape[0] // n_piece
+    w_copies = [pltpu.make_async_copy(w_hbm.at[pl.ds(j * per_piece, per_piece)],
+                                      w_ref.at[pl.ds(j * per_piece, per_piece)], w_sem.at[j])
+                for j in range(n_piece)]
+    for cp in w_copies:
+        cp.start()
     s = lax.axis_index("section")
     d = lax.axis_index("blk")
     nb = pend_ref.shape[0]
@@ -93,7 +101,12 @@
             acc = acc + b_ref[i]
             out_ref[t, i, pl.ds(c * rc, rc)] = jnp.maximum(acc, 0.0).astype(out_ref.dtype)
             return carry
-        lax.fori_loop(0, nb, row_body, 0, unroll=8)
+        if t == 0 and c == 0:
+            for j in range(n_piece):
+                w_copies[j].wait()
+                lax.fori_loop(j * per_piece, (j + 1) * per_piece, row_body, 0, unroll=8)
+        else:
+            lax.fori_loop(0, nb, row_body, 0, unroll=8)
 
     for t in range(TICKS):
         for c in range(n_chunk):
@@ -155,11 +168,13 @@
         in_specs=[
             pl.BlockSpec(memory_space=pltpu.SMEM),
             pl.BlockSpec(memory_space=pltpu.VMEM),
-            pl.BlockSpec(memory_space=pltpu.VMEM),
+            pl.BlockSpec(memory_space=pl.ANY),
             pl.BlockSpec(memory_space=pltpu.VMEM),
         ],
         out_specs=pl.BlockSpec(memory_space=pltpu.VMEM),
         scratch_shapes=[
+            pltpu.VMEM((nb, nz * BLK, BLK), jnp.bfloat16),
+            pltpu.SemaphoreType.DMA((W_PIECES,)),
             pltpu.VMEM((TICKS, npad, rows, BLK), jnp.bfloat16),
             pltpu.SemaphoreType.DMA((TICKS, n_chunk, 3)),
             pltpu.SemaphoreType.DMA((TICKS, n_chunk, 3)),

time: 111 us -> 108 us (0.973)
  Pallas kernels: 106 us -> 103 us
    pallas_call x1, Pallas kernels: 106 us -> 103 us  [shards(): pl.pallas_call(functools.partial(relay_kernel, n_sec, n_blk, n_chunk), ou...]
where the time goes in v5:
time: 108 us
  Pallas kernels  103 us (95%)
  local copies, waits for them, and re-layouts  4.57 us (4%)
    pallas_call x1, Pallas kernels, shards(): pl.pallas_call(functools.partial(relay_kernel, n_sec, n_blk, n_chunk), ou...  103 us
    reshape x1, local copies, waits for them, and re-layouts, shards(): return out.transpose(0, 2, 1, 3).reshape(TICKS, rows, nb * BLK)  2.68 us

profile of v5, /device:TPU:16, one launch (start us, length us, event | category | flops | bytes accessed | tf_op | source)
XLA Modules:
  0.0 108.0 jit_solution(15279867014778832303)
XLA Ops:
  0.0 0.0 copy-start
  0.0 0.8 copy.9
  0.8 0.2 copy-done
  1.1 0.1 bitcast_bitcast_fusion.pend_ref
  1.2 0.0 copy-start.1
  1.2 0.7 copy-done.1
  1.9 103.4 %shard_map.46 = bf16[8,32,64,128]{3,2,1,0:T(8,128)(2,1)S(1)} custom-call(s32[32,8]{1,0:T(8,128)S(1)} %add_select_fusion.cols_ref, bf16[32,64,128]{2,1,0:T(8,128)(2,1)S(1)} %bitcast_bitcast_fusion.pend_ref, bf16[32,1024,128]{2,1,0:T(8,128)(2,1)} %bitcast.20, f32[32,1,128]{2,1,0:T(1,128)S(1)} %bitcast.19), custom_call_target="tpu_custom_call" | custom-call | tf_op jit(solution)/shard_map/pallas_call | solution.py:165
  105.3 2.7 %copy_bitcast_fusion = bf16[8,64,4096]{2,1,0:T(8,128)(2,1)} fusion(bf16[8,32,64,128]{3,2,1,0:T(8,128)(2,1)S(1)} %shard_map.46), kind=kLoop, calls=%fused_computation | loop fusion | bytes 8388608 | tf_op jit(solution)/shard_map/reshape | solution.py:186
  (1 shorter events, 0.0 us)
Async XLA Ops:
  0.0 1.1 copy-start
  1.2 0.7 copy-start.1

commit v6 on v5

--- a/solution.py
+++ b/solution.py
@@ -15,13 +15,15 @@
 MESH = pl.DeviceIdType.MESH
 
 
-def relay_kernel(n_sec, n_blk, n_chunk, cols_ref, pend_ref, w_hbm, b_ref, out_ref,
-                 w_ref, w_sem, slots, send_sem, recv_sem, local_sem, *works):
+def relay_kernel(n_sec, n_blk, n_chunk, src_ref, pend_ref, w_hbm, b_hbm, out_ref,
+                 w_ref, w_sem, b_ref, sendbuf, slots, send_sem, recv_sem, local_sem, *works):
     n_piece = w_sem.shape[0]
     per_piece = w_hbm.shape[0] // n_piece
     w_copies = [pltpu.make_async_copy(w_hbm.at[pl.ds(j * per_piece, per_piece)],
                                       w_ref.at[pl.ds(j * per_piece, per_piece)], w_sem.at[j])
                 for j in range(n_piece)]
+    b_copy = pltpu.make_async_copy(b_hbm, b_ref, local_sem.at[3])
+    b_copy.start()
     for cp in w_copies:
         cp.start()
     s = lax.axis_index("section")
@@ -33,6 +35,9 @@
     s_next = jnp.minimum(s + 1, n_sec - 1)
     s_prev = jnp.maximum(s - 1, 0)
 
+    n_cols = nb * n_blk
+    col_shift = n_cols - d * nb + HALO
+    n_pad = nb + 2 * HALO
     barrier = pltpu.get_barrier_semaphore()
     for nd in (left, right):
         pl.semaphore_signal(barrier, inc=1, device_id=(s, nd), device_id_type=MESH)
@@ -52,7 +57,7 @@
     def center_copy(t, c):
         rows = pl.ds(c * rc, rc)
         return pltpu.make_async_remote_copy(
-            src_ref=out_ref.at[t - 1, :, rows],
+            src_ref=sendbuf.at[t - 1, :, rows],
             dst_ref=slots.at[t, pl.ds(HALO, nb), rows],
             send_sem=send_sem.at[t, c, 0], recv_sem=recv_sem.at[t, c, 0],
             device_id=(s_next, d), device_id_type=MESH)
@@ -95,13 +100,17 @@
         work = works[c]
 
         def row_body(i, carry):
-            xs = [work[cols_ref[i, k]] for k in range(w_ref.shape[1] // BLK)]
+            xs = [work[jnp.minimum(lax.rem(src_ref[i, k] + col_shift, n_cols), n_pad - 1)]
+                  for k in range(w_ref.shape[1] // BLK)]
             xcat = jnp.concatenate(xs, axis=1)
             acc = jnp.dot(xcat, w_ref[i], preferred_element_type=jnp.float32)
             acc = acc + b_ref[i]
-            out_ref[t, i, pl.ds(c * rc, rc)] = jnp.maximum(acc, 0.0).astype(out_ref.dtype)
+            y = jnp.maximum(acc, 0.0).astype(out_ref.dtype)
+            sendbuf[t, i, pl.ds(c * rc, rc)] = y
+            out_ref[t, pl.ds(c * rc, rc), pl.ds(pl.multiple_of(i * BLK, BLK), BLK)] = y
             return carry
         if t == 0 and c == 0:
+            b_copy.wait()
             for j in range(n_piece):
                 w_copies[j].wait()
                 lax.fori_loop(j * per_piece, (j + 1) * per_piece, row_body, 0, unroll=8)
@@ -129,7 +138,7 @@
 
             @pl.when(s < t)
             def _():
-                out_ref[t, :, pl.ds(c * rc, rc)] = jnp.zeros((nb, rc, BLK), out_ref.dtype)
+                out_ref[t, pl.ds(c * rc, rc)] = jnp.zeros((rc, nb * BLK), out_ref.dtype)
 
             if t + 1 < TICKS:
                 @pl.when((s >= t) & (s < n_sec - 1))
@@ -156,34 +165,33 @@
     rows, units = pending_groups.shape
     nb = coefficient_tiles.shape[1]
     nz = coefficient_tiles.shape[2]
-    d = lax.axis_index("blk")
-    cols = jnp.mod(source_block_indices[0] - d * nb + HALO, nb * n_blk).astype(jnp.int32)
     pend = pending_groups.reshape(rows, nb, BLK).transpose(1, 0, 2)
     w = coefficient_tiles[0].reshape(nb, nz * BLK, BLK)
     bias = additive_offsets[0].reshape(nb, 1, BLK)
     npad = nb + 2 * HALO
-    out = pl.pallas_call(
+    return pl.pallas_call(
         functools.partial(relay_kernel, n_sec, n_blk, n_chunk),
-        out_shape=jax.ShapeDtypeStruct((TICKS, nb, rows, BLK), jnp.bfloat16),
+        out_shape=jax.ShapeDtypeStruct((TICKS, rows, nb * BLK), jnp.bfloat16),
         in_specs=[
             pl.BlockSpec(memory_space=pltpu.SMEM),
             pl.BlockSpec(memory_space=pltpu.VMEM),
             pl.BlockSpec(memory_space=pl.ANY),
-            pl.BlockSpec(memory_space=pltpu.VMEM),
+            pl.BlockSpec(memory_space=pl.ANY),
         ],
         out_specs=pl.BlockSpec(memory_space=pltpu.VMEM),
         scratch_shapes=[
             pltpu.VMEM((nb, nz * BLK, BLK), jnp.bfloat16),
             pltpu.SemaphoreType.DMA((W_PIECES,)),
+            pltpu.VMEM((nb, 1, BLK), jnp.float32),
+            pltpu.VMEM((TICKS, nb, rows, BLK), jnp.bfloat16),
             pltpu.VMEM((TICKS, npad, rows, BLK), jnp.bfloat16),
             pltpu.SemaphoreType.DMA((TICKS, n_chunk, 3)),
             pltpu.SemaphoreType.DMA((TICKS, n_chunk, 3)),
-            pltpu.SemaphoreType.DMA((3,)),
+            pltpu.SemaphoreType.DMA((4,)),
         ] + [pltpu.VMEM((npad, rows // n_chunk, BLK), jnp.bfloat16) for _ in range(n_chunk)],
         compiler_params=pltpu.CompilerParams(
             collective_id=0, has_side_effects=True, vmem_limit_bytes=48 * 1024 * 1024),
-    )(cols, pend, w, bias)
-    return out.transpose(0, 2, 1, 3).reshape(TICKS, rows, nb * BLK)
+    )(source_block_indices[0], pend, w, bias)
 
 
 def solution(mesh):

time: 108 us -> 108 us (level)
    reshape x1 -> x0, local copies, waits for them, and re-layouts: 2.68 us -> none  [shards(): return out.transpose(0, 2, 1, 3).reshape(TICKS, rows, nb * BLK)]
    unnamed x5 -> x6, local copies, waits for them, and re-layouts: 1.75 us -> 3.79 us
where the time goes in v6:
time: 108 us
  Pallas kernels  104 us (96%)
  local copies, waits for them, and re-layouts  3.92 us (4%)
    pallas_call x1, Pallas kernels, shards(): pl.pallas_call(functools.partial(relay_kernel, n_sec, n_blk, n_chunk), ou...  104 us
    unnamed x6, local copies, waits for them, and re-layouts  3.79 us

profile of v6, /device:TPU:16, one launch (start us, length us, event | category | flops | bytes accessed | tf_op | source)
XLA Modules:
  0.0 107.6 jit_solution(719559372684471687)
XLA Ops:
  0.0 0.0 copy-start
  0.0 0.8 copy.6
  0.8 0.2 copy-done
  1.1 0.1 bitcast_bitcast_fusion.pend_ref
  1.2 0.0 copy-start.1
  1.2 0.7 copy-done.1
  1.9 103.7 %shard_map.46 = bf16[8,64,4096]{2,1,0:T(8,128)(2,1)S(1)} custom-call(s32[32,8]{1,0:T(8,128)S(1)} %bitcast.10, bf16[32,64,128]{2,1,0:T(8,128)(2,1)S(1)} %bitcast_bitcast_fusion.pend_ref, bf16[32,1024,128]{2,1,0:T(8,128)(2,1)} %bitcast.12, f32[32,1,128]{2,1,0:T(1,128)S(1)} %bitcast.11), custom_call_target="tpu_custom_call" | custom-call | tf_op jit(solution)/shard_map/pallas_call | solution.py:172
  105.6 2.0 %copy.11 = bf16[8,64,4096]{2,1,0:T(8,128)(2,1)} copy(bf16[8,64,4096]{2,1,0:T(8,128)(2,1)S(1)} %shard_map.46) | data formatting | bytes 8388608
Async XLA Ops:
  0.0 1.1 copy-start
  1.2 0.7 copy-start.1

commit v7 on v6

--- a/solution.py
+++ b/solution.py
@@ -54,13 +54,14 @@
     has_next = (2 * n_sec - 3 - s) // (n_sec - 1)
     pl.semaphore_wait(barrier, 2 + has_prev + has_next)
 
-    def center_copy(t, c):
+    def center_copies(t, c):
         rows = pl.ds(c * rc, rc)
-        return pltpu.make_async_remote_copy(
-            src_ref=sendbuf.at[t - 1, :, rows],
-            dst_ref=slots.at[t, pl.ds(HALO, nb), rows],
-            send_sem=send_sem.at[t, c, 0], recv_sem=recv_sem.at[t, c, 0],
-            device_id=(s_next, d), device_id_type=MESH)
+        parts = ((3, 0, HALO), (4, nb - HALO, HALO), (0, HALO, nb - 2 * HALO))
+        return [pltpu.make_async_remote_copy(
+            src_ref=sendbuf.at[t - 1, pl.ds(lo, n), rows],
+            dst_ref=slots.at[t, pl.ds(HALO + lo, n), rows],
+            send_sem=send_sem.at[t, c, j], recv_sem=recv_sem.at[t, c, j],
+            device_id=(s_next, d), device_id_type=MESH) for j, lo, n in parts]
 
     def edge_copies(src, t, c):
         rows = pl.ds(c * rc, rc)
@@ -122,10 +123,13 @@
             if t > 0:
                 @pl.when(s >= t)
                 def _():
-                    center_copy(t, c).wait_recv()
+                    parts = center_copies(t, c)
+                    parts[0].wait_recv()
+                    parts[1].wait_recv()
                     fwd = edge_copies(slots.at[t, pl.ds(HALO, nb)], t, c)
                     for cp in fwd:
                         cp.start()
+                    parts[2].wait_recv()
                     for cp in fwd:
                         cp.wait_recv()
                     cw = pltpu.make_async_copy(slots.at[t, :, pl.ds(c * rc, rc)], works[c], local_sem.at[0])
@@ -143,7 +147,8 @@
             if t + 1 < TICKS:
                 @pl.when((s >= t) & (s < n_sec - 1))
                 def _():
-                    center_copy(t + 1, c).start()
+                    for cp in center_copies(t + 1, c):
+                        cp.start()
 
     for pair in first:
         for cp in pair:
@@ -152,7 +157,8 @@
         @pl.when((s >= t) & (s < n_sec - 1))
         def _():
             for c in range(n_chunk):
-                center_copy(t + 1, c).wait_send()
+                for cp in center_copies(t + 1, c):
+                    cp.wait_send()
     for t in range(1, TICKS):
         @pl.when(s >= t)
         def _():
@@ -185,8 +191,8 @@
             pltpu.VMEM((nb, 1, BLK), jnp.float32),
             pltpu.VMEM((TICKS, nb, rows, BLK), jnp.bfloat16),
             pltpu.VMEM((TICKS, npad, rows, BLK), jnp.bfloat16),
-            pltpu.SemaphoreType.DMA((TICKS, n_chunk, 3)),
-            pltpu.SemaphoreType.DMA((TICKS, n_chunk, 3)),
+            pltpu.SemaphoreType.DMA((TICKS, n_chunk, 5)),
+            pltpu.SemaphoreType.DMA((TICKS, n_chunk, 5)),
             pltpu.SemaphoreType.DMA((4,)),
         ] + [pltpu.VMEM((npad, rows // n_chunk, BLK), jnp.bfloat16) for _ in range(n_chunk)],
         compiler_params=pltpu.CompilerParams(

time: 108 us -> 103 us (0.954)
  Pallas kernels: 104 us -> 98.9 us
    pallas_call x1, Pallas kernels: 104 us -> 98.9 us  [shards(): pl.pallas_call(functools.partial(relay_kernel, n_sec, n_blk, n_chunk), ou...]
where the time goes in v7:
time: 103 us
  Pallas kernels  98.9 us (96%)
  local copies, waits for them, and re-layouts  3.92 us (4%)
    pallas_call x1, Pallas kernels, shards(): pl.pallas_call(functools.partial(relay_kernel, n_sec, n_blk, n_chunk), ou...  98.9 us
    unnamed x6, local copies, waits for them, and re-layouts  3.79 us

profile of v7, /device:TPU:16, one launch (start us, length us, event | category | flops | bytes accessed | tf_op | source)
XLA Modules:
  0.0 102.9 jit_solution(1361486790906575463)
XLA Ops:
  0.0 0.0 copy-start
  0.0 0.8 copy.6
  0.8 0.2 copy-done
  1.1 0.1 bitcast_bitcast_fusion.pend_ref
  1.2 0.0 copy-start.1
  1.2 0.7 copy-done.1
  1.9 98.9 %shard_map.46 = bf16[8,64,4096]{2,1,0:T(8,128)(2,1)S(1)} custom-call(s32[32,8]{1,0:T(8,128)S(1)} %bitcast.10, bf16[32,64,128]{2,1,0:T(8,128)(2,1)S(1)} %bitcast_bitcast_fusion.pend_ref, bf16[32,1024,128]{2,1,0:T(8,128)(2,1)} %bitcast.12, f32[32,1,128]{2,1,0:T(1,128)S(1)} %bitcast.11), custom_call_target="tpu_custom_call" | custom-call | tf_op jit(solution)/shard_map/pallas_call | solution.py:178
  100.8 2.0 %copy.11 = bf16[8,64,4096]{2,1,0:T(8,128)(2,1)} copy(bf16[8,64,4096]{2,1,0:T(8,128)(2,1)S(1)} %shard_map.46) | data formatting | bytes 8388608
Async XLA Ops:
  0.0 1.1 %copy-start = (bf16[64,4096]{1,0:T(8,128)(2,1)S(1)}, bf16[64,4096]{1,0:T(8,128)(2,1)}, u32[]{:S(2)}) copy-start(bf16[64,4096]{1,0:T(8,128)(2,1)} %param.4) | copy-start | bytes 1572868
  1.2 0.7 copy-start.1

commit v8 on v7

--- a/solution.py
+++ b/solution.py
@@ -16,7 +16,7 @@
 
 
 def relay_kernel(n_sec, n_blk, n_chunk, src_ref, pend_ref, w_hbm, b_hbm, out_ref,
-                 w_ref, w_sem, b_ref, sendbuf, slots, send_sem, recv_sem, local_sem, *works):
+                 w_ref, w_sem, b_ref, sendbuf, send_sem, recv_sem, local_sem, *slot_list):
     n_piece = w_sem.shape[0]
     per_piece = w_hbm.shape[0] // n_piece
     w_copies = [pltpu.make_async_copy(w_hbm.at[pl.ds(j * per_piece, per_piece)],
@@ -26,6 +26,7 @@
     b_copy.start()
     for cp in w_copies:
         cp.start()
+    slots = [slot_list[t * n_chunk:(t + 1) * n_chunk] for t in range(TICKS)]
     s = lax.axis_index("section")
     d = lax.axis_index("blk")
     nb = pend_ref.shape[0]
@@ -59,46 +60,37 @@
         parts = ((3, 0, HALO), (4, nb - HALO, HALO), (0, HALO, nb - 2 * HALO))
         return [pltpu.make_async_remote_copy(
             src_ref=sendbuf.at[t - 1, pl.ds(lo, n), rows],
-            dst_ref=slots.at[t, pl.ds(HALO + lo, n), rows],
+            dst_ref=slots[t][c].at[pl.ds(HALO + lo, n)],
             send_sem=send_sem.at[t, c, j], recv_sem=recv_sem.at[t, c, j],
             device_id=(s_next, d), device_id_type=MESH) for j, lo, n in parts]
 
     def edge_copies(src, t, c):
-        rows = pl.ds(c * rc, rc)
         lo = pltpu.make_async_remote_copy(
-            src_ref=src.at[pl.ds(0, HALO), rows],
-            dst_ref=slots.at[t, pl.ds(HALO + nb, HALO), rows],
+            src_ref=src.at[pl.ds(0, HALO)],
+            dst_ref=slots[t][c].at[pl.ds(HALO + nb, HALO)],
             send_sem=send_sem.at[t, c, 1], recv_sem=recv_sem.at[t, c, 1],
             device_id=(s, left), device_id_type=MESH)
         hi = pltpu.make_async_remote_copy(
-            src_ref=src.at[pl.ds(nb - HALO, HALO), rows],
-            dst_ref=slots.at[t, pl.ds(0, HALO), rows],
+            src_ref=src.at[pl.ds(nb - HALO, HALO)],
+            dst_ref=slots[t][c].at[pl.ds(0, HALO)],
             send_sem=send_sem.at[t, c, 2], recv_sem=recv_sem.at[t, c, 2],
             device_id=(s, right), device_id_type=MESH)
         return lo, hi
 
-    first = [edge_copies(pend_ref, 0, c) for c in range(n_chunk)]
+    first = [edge_copies(pend_ref.at[:, pl.ds(c * rc, rc)], 0, c) for c in range(n_chunk)]
     for pair in first:
         for cp in pair:
             cp.start()
     for c in range(n_chunk):
-        rows = pl.ds(c * rc, rc)
-        own = pltpu.make_async_copy(pend_ref.at[:, rows], works[c].at[pl.ds(HALO, nb)], local_sem.at[0])
+        own = pltpu.make_async_copy(pend_ref.at[:, pl.ds(c * rc, rc)], slots[0][c].at[pl.ds(HALO, nb)],
+                                    local_sem.at[0])
         own.start()
         own.wait()
         for cp in first[c]:
             cp.wait_recv()
-        cp_lo = pltpu.make_async_copy(slots.at[0, pl.ds(0, HALO), rows], works[c].at[pl.ds(0, HALO)],
-                                      local_sem.at[1])
-        cp_hi = pltpu.make_async_copy(slots.at[0, pl.ds(HALO + nb, HALO), rows],
-                                      works[c].at[pl.ds(HALO + nb, HALO)], local_sem.at[2])
-        cp_lo.start()
-        cp_hi.start()
-        cp_lo.wait()
-        cp_hi.wait()
 
     def compute(t, c):
-        work = works[c]
+        work = slots[t][c]
 
         def row_body(i, carry):
             xs = [work[jnp.minimum(lax.rem(src_ref[i, k] + col_shift, n_cols), n_pad - 1)]
@@ -126,15 +118,12 @@
                     parts = center_copies(t, c)
                     parts[0].wait_recv()
                     parts[1].wait_recv()
-                    fwd = edge_copies(slots.at[t, pl.ds(HALO, nb)], t, c)
+                    fwd = edge_copies(slots[t][c].at[pl.ds(HALO, nb)], t, c)
                     for cp in fwd:
                         cp.start()
                     parts[2].wait_recv()
                     for cp in fwd:
                         cp.wait_recv()
-                    cw = pltpu.make_async_copy(slots.at[t, :, pl.ds(c * rc, rc)], works[c], local_sem.at[0])
-                    cw.start()
-                    cw.wait()
 
             @pl.when(s >= t)
             def _():
@@ -163,7 +152,7 @@
         @pl.when(s >= t)
         def _():
             for c in range(n_chunk):
-                for cp in edge_copies(slots.at[t, pl.ds(HALO, nb)], t, c):
+                for cp in edge_copies(slots[t][c].at[pl.ds(HALO, nb)], t, c):
                     cp.wait_send()
 
 
@@ -190,11 +179,10 @@
             pltpu.SemaphoreType.DMA((W_PIECES,)),
             pltpu.VMEM((nb, 1, BLK), jnp.float32),
             pltpu.VMEM((TICKS, nb, rows, BLK), jnp.bfloat16),
-            pltpu.VMEM((TICKS, npad, rows, BLK), jnp.bfloat16),
             pltpu.SemaphoreType.DMA((TICKS, n_chunk, 5)),
             pltpu.SemaphoreType.DMA((TICKS, n_chunk, 5)),
             pltpu.SemaphoreType.DMA((4,)),
-        ] + [pltpu.VMEM((npad, rows // n_chunk, BLK), jnp.bfloat16) for _ in range(n_chunk)],
+        ] + [pltpu.VMEM((npad, rows // n_chunk, BLK), jnp.bfloat16) for _ in range(TICKS * n_chunk)],
         compiler_params=pltpu.CompilerParams(
             collective_id=0, has_side_effects=True, vmem_limit_bytes=48 * 1024 * 1024),
     )(source_block_indices[0], pend, w, bias)

time: 103 us -> 103 us (level)
  no operation moved by 1% of the time
where the time goes in v8:
time: 103 us
  Pallas kernels  98.9 us (96%)
  local copies, waits for them, and re-layouts  3.92 us (4%)
    pallas_call x1, Pallas kernels, shards(): pl.pallas_call(functools.partial(relay_kernel, n_sec, n_blk, n_chunk), ou...  98.9 us
    unnamed x6, local copies, waits for them, and re-layouts  3.79 us

profile of v8, /device:TPU:16, one launch (start us, length us, event | category | flops | bytes accessed | tf_op | source)
XLA Modules:
  0.0 102.8 jit_solution(3238387867150905996)
XLA Ops:
  0.0 0.0 copy-start
  0.0 0.8 copy.6
  0.8 0.2 copy-done
  1.1 0.1 bitcast_bitcast_fusion.pend_ref
  1.2 0.0 copy-start.1
  1.2 0.7 copy-done.1
  1.9 98.9 %shard_map.46 = bf16[8,64,4096]{2,1,0:T(8,128)(2,1)S(1)} custom-call(s32[32,8]{1,0:T(8,128)S(1)} %bitcast.10, bf16[32,64,128]{2,1,0:T(8,128)(2,1)S(1)} %bitcast_bitcast_fusion.pend_ref, bf16[32,1024,128]{2,1,0:T(8,128)(2,1)} %bitcast.12, f32[32,1,128]{2,1,0:T(1,128)S(1)} %bitcast.11), custom_call_target="tpu_custom_call" | custom-call | tf_op jit(solution)/shard_map/pallas_call | solution.py:167
  100.8 2.0 %copy.11 = bf16[8,64,4096]{2,1,0:T(8,128)(2,1)} copy(bf16[8,64,4096]{2,1,0:T(8,128)(2,1)S(1)} %shard_map.46) | data formatting | bytes 8388608
Async XLA Ops:
  0.0 1.1 %copy-start = (bf16[64,4096]{1,0:T(8,128)(2,1)S(1)}, bf16[64,4096]{1,0:T(8,128)(2,1)}, u32[]{:S(2)}) copy-start(bf16[64,4096]{1,0:T(8,128)(2,1)} %param.4) | copy-start | bytes 1572868
  1.2 0.7 copy-start.1

commit v9 on v8

--- a/solution.py
+++ b/solution.py
@@ -12,6 +12,7 @@
 TICKS = 8
 ROW_CHUNKS = 2
 W_PIECES = 4
+VMEM_BYTES = 67043328
 MESH = pl.DeviceIdType.MESH
 
 
@@ -93,7 +94,7 @@
         work = slots[t][c]
 
         def row_body(i, carry):
-            xs = [work[jnp.minimum(lax.rem(src_ref[i, k] + col_shift, n_cols), n_pad - 1)]
+            xs = [work[jnp.minimum(lax.rem(src_ref[k, i] + col_shift, n_cols), n_pad - 1)]
                   for k in range(w_ref.shape[1] // BLK)]
             xcat = jnp.concatenate(xs, axis=1)
             acc = jnp.dot(xcat, w_ref[i], preferred_element_type=jnp.float32)
@@ -184,8 +185,8 @@
             pltpu.SemaphoreType.DMA((4,)),
         ] + [pltpu.VMEM((npad, rows // n_chunk, BLK), jnp.bfloat16) for _ in range(TICKS * n_chunk)],
         compiler_params=pltpu.CompilerParams(
-            collective_id=0, has_side_effects=True, vmem_limit_bytes=48 * 1024 * 1024),
-    )(source_block_indices[0], pend, w, bias)
+            collective_id=0, has_side_effects=True, vmem_limit_bytes=VMEM_BYTES),
+    )(source_block_indices[0].T, pend, w, bias)
 
 
 def solution(mesh):

time: 103 us -> 108 us (1.049)
  local copies, waits for them, and re-layouts: 3.92 us -> 6.68 us
  Pallas kernels: 98.9 us -> 101 us
    pallas_call x1, Pallas kernels: 98.9 us -> 101 us  [shards(): pl.pallas_call(functools.partial(relay_kernel, n_sec, n_blk, n_chunk), ou...]
    transpose x1, local copies, waits for them, and re-layouts: 0.13 us -> 1.98 us  [shards(): pend = pending_groups.reshape(rows, nb, BLK).transpose(1, 0, 2)]
    unnamed x6 -> x1, local copies, waits for them, and re-layouts: 3.79 us -> 4.7 us
where the time goes in v9:
time: 108 us
  Pallas kernels  101 us (94%)
  local copies, waits for them, and re-layouts  6.68 us (6%)
    pallas_call x1, Pallas kernels, shards(): pl.pallas_call(functools.partial(relay_kernel, n_sec, n_blk, n_chunk), ou...  101 us
    unnamed x1, local copies, waits for them, and re-layouts  4.7 us

profile of v9, /device:TPU:16, one launch (start us, length us, event | category | flops | bytes accessed | tf_op | source)
XLA Modules:
  0.0 107.7 jit_solution(11730589074635299734)
XLA Ops:
  0.0 2.0 %bitcast_bitcast_fusion.pend_ref = bf16[32,64,128]{2,1,0:T(8,128)(2,1)} fusion(bf16[64,4096]{1,0:T(8,128)(2,1)} %param.4), kind=kLoop, calls=%fused_computation | loop fusion | bytes 1048576 | tf_op jit(solution)/shard_map/transpose | solution.py:164
  2.0 101.0 %shard_map.46 = bf16[8,64,4096]{2,1,0:T(8,128)(2,1)} custom-call(s32[8,32]{1,0:T(8,128)} %bitcast.14, bf16[32,64,128]{2,1,0:T(8,128)(2,1)} %bitcast_bitcast_fusion.pend_ref, bf16[32,1024,128]{2,1,0:T(8,128)(2,1)} %bitcast.12, f32[32,1,128]{2,1,0:T(1,128)} %bitcast.13), custom_call_target="tpu_custom_call" | custom-call | tf_op jit(solution)/shard_map/pallas_call | solution.py:168
  103.0 4.7 %copy.9 = bf16[8,64,4096]{2,1,0:T(8,128)(2,1)} copy(bf16[8,64,4096]{2,1,0:T(8,128)(2,1)} %shard_map.46) | data formatting | bytes 8388608

commit v10 on v9

--- a/solution.py
+++ b/solution.py
@@ -12,7 +12,7 @@
 TICKS = 8
 ROW_CHUNKS = 2
 W_PIECES = 4
-VMEM_BYTES = 67043328
+VMEM_BYTES = 48 * 1024 * 1024
 MESH = pl.DeviceIdType.MESH
 
 

time: 108 us -> 103 us (0.954)
  Pallas kernels: 101 us -> 98.7 us
  local copies, waits for them, and re-layouts: 6.68 us -> 4.59 us
    pallas_call x1, Pallas kernels: 101 us -> 98.7 us  [shards(): pl.pallas_call(functools.partial(relay_kernel, n_sec, n_blk, n_chunk), ou...]
    transpose x1, local copies, waits for them, and re-layouts: 1.98 us -> 0.13 us  [shards(): pend = pending_groups.reshape(rows, nb, BLK).transpose(1, 0, 2)]
    unnamed x1 -> x7, local copies, waits for them, and re-layouts: 4.7 us -> 4.46 us
where the time goes in v10:
time: 103 us
  Pallas kernels  98.7 us (96%)
  local copies, waits for them, and re-layouts  4.59 us (4%)
    pallas_call x1, Pallas kernels, shards(): pl.pallas_call(functools.partial(relay_kernel, n_sec, n_blk, n_chunk), ou...  98.7 us
    unnamed x7, local copies, waits for them, and re-layouts  4.46 us

profile of v10, /device:TPU:16, one launch (start us, length us, event | category | flops | bytes accessed | tf_op | source)
XLA Modules:
  0.0 103.3 jit_solution(784136295555902836)
XLA Ops:
  0.0 0.0 copy-start
  0.0 1.0 %copy-done = bf16[64,4096]{1,0:T(8,128)(2,1)S(1)} copy-done((bf16[64,4096]{1,0:T(8,128)(2,1)S(1)}, bf16[64,4096]{1,0:T(8,128)(2,1)}, u32[]{:S(2)}) %copy-start) | copy-done | bytes 524312
  1.0 0.1 bitcast_bitcast_fusion.pend_ref
  1.2 0.0 copy-start.1
  1.2 0.7 copy-done.1
  1.9 0.0 copy-start.2
  1.9 0.7 copy-done.2
  2.6 98.7 %shard_map.46 = bf16[8,64,4096]{2,1,0:T(8,128)(2,1)S(1)} custom-call(s32[8,32]{1,0:T(8,128)S(1)} %bitcast.13, bf16[32,64,128]{2,1,0:T(8,128)(2,1)S(1)} %bitcast_bitcast_fusion.pend_ref, bf16[32,1024,128]{2,1,0:T(8,128)(2,1)} %bitcast.14, f32[32,1,128]{2,1,0:T(1,128)S(1)} %bitcast.12), custom_call_target="tpu_custom_call" | custom-call | tf_op jit(solution)/shard_map/pallas_call | solution.py:168
  101.3 2.0 %copy.9 = bf16[8,64,4096]{2,1,0:T(8,128)(2,1)} copy(bf16[8,64,4096]{2,1,0:T(8,128)(2,1)S(1)} %shard_map.46) | data formatting | bytes 8388608
Async XLA Ops:
  0.0 1.0 %copy-start = (bf16[64,4096]{1,0:T(8,128)(2,1)S(1)}, bf16[64,4096]{1,0:T(8,128)(2,1)}, u32[]{:S(2)}) copy-start(bf16[64,4096]{1,0:T(8,128)(2,1)} %param.4) | copy-start | bytes 1572868
  1.2 0.7 copy-start.1
  1.9 0.7 copy-start.2

commit v11 on v10

--- a/solution.py
+++ b/solution.py
@@ -109,7 +109,7 @@
                 w_copies[j].wait()
                 lax.fori_loop(j * per_piece, (j + 1) * per_piece, row_body, 0, unroll=8)
         else:
-            lax.fori_loop(0, nb, row_body, 0, unroll=8)
+            lax.fori_loop(0, nb, row_body, 0, unroll=True)
 
     for t in range(TICKS):
         for c in range(n_chunk):

time: 103 us -> 103 us (level)
  no operation moved by 1% of the time
where the time goes in v11:
time: 103 us
  Pallas kernels  98 us (95%)
  local copies, waits for them, and re-layouts  4.59 us (4%)
    pallas_call x1, Pallas kernels, shards(): pl.pallas_call(functools.partial(relay_kernel, n_sec, n_blk, n_chunk), ou...  98 us
    unnamed x7, local copies, waits for them, and re-layouts  4.46 us

profile of v11, /device:TPU:16, one launch (start us, length us, event | category | flops | bytes accessed | tf_op | source)
XLA Modules:
  0.0 102.6 jit_solution(17275315472850709762)
XLA Ops:
  0.0 0.0 copy-start
  0.0 1.0 %copy-done = bf16[64,4096]{1,0:T(8,128)(2,1)S(1)} copy-done((bf16[64,4096]{1,0:T(8,128)(2,1)S(1)}, bf16[64,4096]{1,0:T(8,128)(2,1)}, u32[]{:S(2)}) %copy-start) | copy-done | bytes 524312
  1.0 0.1 bitcast_bitcast_fusion.pend_ref
  1.2 0.0 copy-start.1
  1.2 0.7 copy-done.1
  1.9 0.0 copy-start.2
  1.9 0.7 copy-done.2
  2.6 98.0 %shard_map.46 = bf16[8,64,4096]{2,1,0:T(8,128)(2,1)S(1)} custom-call(s32[8,32]{1,0:T(8,128)S(1)} %bitcast.13, bf16[32,64,128]{2,1,0:T(8,128)(2,1)S(1)} %bitcast_bitcast_fusion.pend_ref, bf16[32,1024,128]{2,1,0:T(8,128)(2,1)} %bitcast.14, f32[32,1,128]{2,1,0:T(1,128)S(1)} %bitcast.12), custom_call_target="tpu_custom_call" | custom-call | tf_op jit(solution)/shard_map/pallas_call | solution.py:168
  100.6 2.0 %copy.9 = bf16[8,64,4096]{2,1,0:T(8,128)(2,1)} copy(bf16[8,64,4096]{2,1,0:T(8,128)(2,1)S(1)} %shard_map.46) | data formatting | bytes 8388608
Async XLA Ops:
  0.0 1.0 %copy-start = (bf16[64,4096]{1,0:T(8,128)(2,1)S(1)}, bf16[64,4096]{1,0:T(8,128)(2,1)}, u32[]{:S(2)}) copy-start(bf16[64,4096]{1,0:T(8,128)(2,1)} %param.4) | copy-start | bytes 1572868
  1.2 0.7 copy-start.1
  1.9 0.7 copy-start.2

commit v12 on v11

--- a/solution.py
+++ b/solution.py
@@ -90,7 +90,14 @@
         for cp in first[c]:
             cp.wait_recv()
 
-    def compute(t, c):
+    def forward_edges(t, c):
+        parts = center_copies(t, c)
+        parts[0].wait_recv()
+        parts[1].wait_recv()
+        for cp in edge_copies(slots[t][c].at[pl.ds(HALO, nb)], t, c):
+            cp.start()
+
+    def compute(t, c, mid=None):
         work = slots[t][c]
 
         def row_body(i, carry):
@@ -108,8 +115,12 @@
             for j in range(n_piece):
                 w_copies[j].wait()
                 lax.fori_loop(j * per_piece, (j + 1) * per_piece, row_body, 0, unroll=8)
+        elif mid is None:
+            lax.fori_loop(0, nb, row_body, 0, unroll=True)
         else:
-            lax.fori_loop(0, nb, row_body, 0, unroll=True)
+            lax.fori_loop(0, nb // 2, row_body, 0, unroll=True)
+            mid()
+            lax.fori_loop(nb // 2, nb, row_body, 0, unroll=True)
 
     for t in range(TICKS):
         for c in range(n_chunk):
@@ -117,18 +128,19 @@
                 @pl.when(s >= t)
                 def _():
                     parts = center_copies(t, c)
-                    parts[0].wait_recv()
-                    parts[1].wait_recv()
                     fwd = edge_copies(slots[t][c].at[pl.ds(HALO, nb)], t, c)
-                    for cp in fwd:
-                        cp.start()
+                    if c == 0:
+                        forward_edges(t, c)
                     parts[2].wait_recv()
                     for cp in fwd:
                         cp.wait_recv()
 
             @pl.when(s >= t)
             def _():
-                compute(t, c)
+                if t > 0 and c + 1 < n_chunk:
+                    compute(t, c, functools.partial(forward_edges, t, c + 1))
+                else:
+                    compute(t, c)
 
             @pl.when(s < t)
             def _():

time: 103 us -> 103 us (level)
  no operation moved by 1% of the time
where the time goes in v12:
time: 103 us
  Pallas kernels  97.9 us (95%)
  local copies, waits for them, and re-layouts  4.59 us (4%)
    pallas_call x1, Pallas kernels, shards(): pl.pallas_call(functools.partial(relay_kernel, n_sec, n_blk, n_chunk), ou...  97.9 us
    unnamed x7, local copies, waits for them, and re-layouts  4.46 us

profile of v12, /device:TPU:16, one launch (start us, length us, event | category | flops | bytes accessed | tf_op | source)
XLA Modules:
  0.0 102.5 jit_solution(14174883801737110696)
XLA Ops:
  0.0 0.0 copy-start
  0.0 1.0 %copy-done = bf16[64,4096]{1,0:T(8,128)(2,1)S(1)} copy-done((bf16[64,4096]{1,0:T(8,128)(2,1)S(1)}, bf16[64,4096]{1,0:T(8,128)(2,1)}, u32[]{:S(2)}) %copy-start) | copy-done | bytes 524312
  1.0 0.1 bitcast_bitcast_fusion.pend_ref
  1.2 0.0 copy-start.1
  1.2 0.7 copy-done.1
  1.9 0.0 copy-start.2
  1.9 0.7 copy-done.2
  2.6 97.9 %shard_map.46 = bf16[8,64,4096]{2,1,0:T(8,128)(2,1)S(1)} custom-call(s32[8,32]{1,0:T(8,128)S(1)} %bitcast.13, bf16[32,64,128]{2,1,0:T(8,128)(2,1)S(1)} %bitcast_bitcast_fusion.pend_ref, bf16[32,1024,128]{2,1,0:T(8,128)(2,1)} %bitcast.14, f32[32,1,128]{2,1,0:T(1,128)S(1)} %bitcast.12), custom_call_target="tpu_custom_call" | custom-call | tf_op jit(solution)/shard_map/pallas_call | solution.py:180
  100.5 2.0 %copy.9 = bf16[8,64,4096]{2,1,0:T(8,128)(2,1)} copy(bf16[8,64,4096]{2,1,0:T(8,128)(2,1)S(1)} %shard_map.46) | data formatting | bytes 8388608
Async XLA Ops:
  0.0 1.0 %copy-start = (bf16[64,4096]{1,0:T(8,128)(2,1)S(1)}, bf16[64,4096]{1,0:T(8,128)(2,1)}, u32[]{:S(2)}) copy-start(bf16[64,4096]{1,0:T(8,128)(2,1)} %param.4) | copy-start | bytes 1572868
  1.2 0.7 copy-start.1
  1.9 0.7 copy-start.2

commit v13 on v11

--- a/solution.py
+++ b/solution.py
@@ -11,7 +11,7 @@
 HALO = 4
 TICKS = 8
 ROW_CHUNKS = 2
-W_PIECES = 4
+W_PIECES = 8
 VMEM_BYTES = 48 * 1024 * 1024
 MESH = pl.DeviceIdType.MESH
 
@@ -28,6 +28,12 @@
     for cp in w_copies:
         cp.start()
     slots = [slot_list[t * n_chunk:(t + 1) * n_chunk] for t in range(TICKS)]
+    rc0 = pend_ref.shape[1] // n_chunk
+    nb0 = pend_ref.shape[0]
+    own = [pltpu.make_async_copy(pend_ref.at[:, pl.ds(c * rc0, rc0)], slots[0][c].at[pl.ds(HALO, nb0)],
+                                 local_sem.at[c]) for c in range(n_chunk)]
+    for cp in own:
+        cp.start()
     s = lax.axis_index("section")
     d = lax.axis_index("blk")
     nb = pend_ref.shape[0]
@@ -82,13 +88,6 @@
     for pair in first:
         for cp in pair:
             cp.start()
-    for c in range(n_chunk):
-        own = pltpu.make_async_copy(pend_ref.at[:, pl.ds(c * rc, rc)], slots[0][c].at[pl.ds(HALO, nb)],
-                                    local_sem.at[0])
-        own.start()
-        own.wait()
-        for cp in first[c]:
-            cp.wait_recv()
 
     def compute(t, c):
         work = slots[t][c]
@@ -113,6 +112,10 @@
 
     for t in range(TICKS):
         for c in range(n_chunk):
+            if t == 0:
+                own[c].wait()
+                for cp in first[c]:
+                    cp.wait_recv()
             if t > 0:
                 @pl.when(s >= t)
                 def _():

time: 103 us -> 106 us (1.029)
  Pallas kernels: 98 us -> 101 us
    pallas_call x1, Pallas kernels: 98 us -> 101 us  [shards(): pl.pallas_call(functools.partial(relay_kernel, n_sec, n_blk, n_chunk), ou...]
where the time goes in v13:
time: 106 us
  Pallas kernels  101 us (95%)
  local copies, waits for them, and re-layouts  4.59 us (4%)
    pallas_call x1, Pallas kernels, shards(): pl.pallas_call(functools.partial(relay_kernel, n_sec, n_blk, n_chunk), ou...  101 us
    unnamed x7, local copies, waits for them, and re-layouts  4.46 us

profile of v13, /device:TPU:16, one launch (start us, length us, event | category | flops | bytes accessed | tf_op | source)
XLA Modules:
  0.0 105.9 jit_solution(8309088692539791806)
XLA Ops:
  0.0 0.0 copy-start
  0.0 1.0 copy-done
  1.0 0.1 bitcast_bitcast_fusion.pend_ref
  1.2 0.0 copy-start.1
  1.2 0.7 copy-done.1
  1.9 0.0 copy-start.2
  1.9 0.7 copy-done.2
  2.6 101.3 %shard_map.46 = bf16[8,64,4096]{2,1,0:T(8,128)(2,1)S(1)} custom-call(s32[8,32]{1,0:T(8,128)S(1)} %bitcast.13, bf16[32,64,128]{2,1,0:T(8,128)(2,1)S(1)} %bitcast_bitcast_fusion.pend_ref, bf16[32,1024,128]{2,1,0:T(8,128)(2,1)} %bitcast.14, f32[32,1,128]{2,1,0:T(1,128)S(1)} %bitcast.12), custom_call_target="tpu_custom_call" | custom-call | tf_op jit(solution)/shard_map/pallas_call | solution.py:171
  103.9 2.0 %copy.9 = bf16[8,64,4096]{2,1,0:T(8,128)(2,1)} copy(bf16[8,64,4096]{2,1,0:T(8,128)(2,1)S(1)} %shard_map.46) | data formatting | bytes 8388608
Async XLA Ops:
  0.0 1.0 copy-start
  1.2 0.7 copy-start.1
  1.9 0.7 copy-start.2

commit v14 on v11

--- a/solution.py
+++ b/solution.py
@@ -11,7 +11,7 @@
 HALO = 4
 TICKS = 8
 ROW_CHUNKS = 2
-W_PIECES = 4
+W_PIECES = 2
 VMEM_BYTES = 48 * 1024 * 1024
 MESH = pl.DeviceIdType.MESH
 

time: 103 us -> 103 us (level)
  no operation moved by 1% of the time
where the time goes in v14:
time: 103 us
  Pallas kernels  97.9 us (95%)
  local copies, waits for them, and re-layouts  4.59 us (4%)
    pallas_call x1, Pallas kernels, shards(): pl.pallas_call(functools.partial(relay_kernel, n_sec, n_blk, n_chunk), ou...  97.9 us
    unnamed x7, local copies, waits for them, and re-layouts  4.46 us

profile of v14, /device:TPU:16, one launch (start us, length us, event | category | flops | bytes accessed | tf_op | source)
XLA Modules:
  0.0 102.5 jit_solution(4675486024703713761)
XLA Ops:
  0.0 0.0 copy-start
  0.0 1.0 %copy-done = bf16[64,4096]{1,0:T(8,128)(2,1)S(1)} copy-done((bf16[64,4096]{1,0:T(8,128)(2,1)S(1)}, bf16[64,4096]{1,0:T(8,128)(2,1)}, u32[]{:S(2)}) %copy-start) | copy-done | bytes 524312
  1.0 0.1 bitcast_bitcast_fusion.pend_ref
  1.2 0.0 copy-start.1
  1.2 0.7 copy-done.1
  1.9 0.0 copy-start.2
  1.9 0.7 copy-done.2
  2.6 97.9 %shard_map.46 = bf16[8,64,4096]{2,1,0:T(8,128)(2,1)S(1)} custom-call(s32[8,32]{1,0:T(8,128)S(1)} %bitcast.13, bf16[32,64,128]{2,1,0:T(8,128)(2,1)S(1)} %bitcast_bitcast_fusion.pend_ref, bf16[32,1024,128]{2,1,0:T(8,128)(2,1)} %bitcast.14, f32[32,1,128]{2,1,0:T(1,128)S(1)} %bitcast.12), custom_call_target="tpu_custom_call" | custom-call | tf_op jit(solution)/shard_map/pallas_call | solution.py:168
  100.5 2.0 %copy.9 = bf16[8,64,4096]{2,1,0:T(8,128)(2,1)} copy(bf16[8,64,4096]{2,1,0:T(8,128)(2,1)S(1)} %shard_map.46) | data formatting | bytes 8388608
Async XLA Ops:
  0.0 1.0 %copy-start = (bf16[64,4096]{1,0:T(8,128)(2,1)S(1)}, bf16[64,4096]{1,0:T(8,128)(2,1)}, u32[]{:S(2)}) copy-start(bf16[64,4096]{1,0:T(8,128)(2,1)} %param.4) | copy-start | bytes 1572868
  1.2 0.7 copy-start.1
  1.9 0.7 copy-start.2

commit v15 on v14

--- a/solution.py
+++ b/solution.py
@@ -107,7 +107,7 @@
             b_copy.wait()
             for j in range(n_piece):
                 w_copies[j].wait()
-                lax.fori_loop(j * per_piece, (j + 1) * per_piece, row_body, 0, unroll=8)
+                lax.fori_loop(j * per_piece, (j + 1) * per_piece, row_body, 0, unroll=True)
         else:
             lax.fori_loop(0, nb, row_body, 0, unroll=True)
 

time: 103 us -> 103 us (level)
  no operation moved by 1% of the time
where the time goes in v15:
time: 103 us; the launch traced here: 102 us
  Pallas kernels  97.7 us (95%)
  local copies, waits for them, and re-layouts  4.59 us (4%)
    pallas_call x1, Pallas kernels, shards(): pl.pallas_call(functools.partial(relay_kernel, n_sec, n_blk, n_chunk), ou...  97.7 us
    unnamed x7, local copies, waits for them, and re-layouts  4.46 us

profile of v15, /device:TPU:16, one launch (start us, length us, event | category | flops | bytes accessed | tf_op | source)
XLA Modules:
  0.0 102.3 jit_solution(2136113328693271873)
XLA Ops:
  0.0 0.0 copy-start
  0.0 1.0 %copy-done = bf16[64,4096]{1,0:T(8,128)(2,1)S(1)} copy-done((bf16[64,4096]{1,0:T(8,128)(2,1)S(1)}, bf16[64,4096]{1,0:T(8,128)(2,1)}, u32[]{:S(2)}) %copy-start) | copy-done | bytes 524312
  1.0 0.1 bitcast_bitcast_fusion.pend_ref
  1.2 0.0 copy-start.1
  1.2 0.7 copy-done.1
  1.9 0.0 copy-start.2
  1.9 0.7 copy-done.2
  2.6 97.7 %shard_map.46 = bf16[8,64,4096]{2,1,0:T(8,128)(2,1)S(1)} custom-call(s32[8,32]{1,0:T(8,128)S(1)} %bitcast.13, bf16[32,64,128]{2,1,0:T(8,128)(2,1)S(1)} %bitcast_bitcast_fusion.pend_ref, bf16[32,1024,128]{2,1,0:T(8,128)(2,1)} %bitcast.14, f32[32,1,128]{2,1,0:T(1,128)S(1)} %bitcast.12), custom_call_target="tpu_custom_call" | custom-call | tf_op jit(solution)/shard_map/pallas_call | solution.py:168
  100.3 2.0 %copy.9 = bf16[8,64,4096]{2,1,0:T(8,128)(2,1)} copy(bf16[8,64,4096]{2,1,0:T(8,128)(2,1)S(1)} %shard_map.46) | data formatting | bytes 8388608
Async XLA Ops:
  0.0 1.0 %copy-start = (bf16[64,4096]{1,0:T(8,128)(2,1)S(1)}, bf16[64,4096]{1,0:T(8,128)(2,1)}, u32[]{:S(2)}) copy-start(bf16[64,4096]{1,0:T(8,128)(2,1)} %param.4) | copy-start | bytes 1572868
  1.2 0.7 copy-start.1
  1.9 0.7 copy-start.2
